TPU v7x, 32 devices: a whole 2x2x4 slice. The times are simulated.
32 devices in a mesh: tm: 4 (over z), space: 8 (over y, x, core).
Axes of the slice: x: 2, y: 2, z: 4, core: 2. Of those that a mesh axis runs over, the one named last changes fastest.
Arguments:
- snapshots: bfloat16 [512, 393216], P('tm', 'space'), may hold values from -10 to 10, as said below
- area_weight: float32 [393216], P('space'), may hold values from 0.1 to 1
- eigvecs: bfloat16 [512, 64], replicated, may hold values from -0.25 to 0.25
- eigvals: float32 [64], replicated, may hold values from 0.5 to 8
Outputs:
- gram: float32 [512, 512], P(('tm', 'space'))
- modes: bfloat16 [64, 393216], P('tm', 'space')
Inputs may be any that keep to these rules, and one draw needn't show every extreme that they name: `snapshots`: a per-column climatology plus hourly departures.
All inputs are finite; a program needn't handle non-finite values.
Results may differ from a plain program's by a relative error of at most 0.01.
Values may be sent and summed in bfloat16 or wider, within the bound.
No kernel may reach another device: no remote copies, remote signals or barrier semaphores. Data moves between devices by JAX's collectives and lax.ppermute only.
A program may use at most 128 MiB of HBM per device.

v0:
```python
import jax
import jax.numpy as jnp
from jax import lax
from jax.sharding import PartitionSpec as P


def gram_local(weighted):
    return lax.dot_general(
        weighted, weighted, (((1,), (1,)), ((), ())), preferred_element_type=jnp.float32
    )


def local(snapshots, area_weight, eigvecs, eigvals):
    tm_count = lax.axis_size("tm")
    space_count = lax.axis_size("space")
    time_dev, cell_dev = snapshots.shape
    times = time_dev * tm_count
    cells = cell_dev * space_count
    sub_cells = cell_dev // tm_count
    tm_index = lax.axis_index("tm")
    columns = lax.all_to_all(snapshots, "tm", split_axis=1, concat_axis=0, tiled=True)
    mean = jnp.sum(columns.astype(jnp.float32), axis=0) / times
    root = jnp.sqrt(area_weight)
    own_root = lax.dynamic_slice_in_dim(root, tm_index * sub_cells, sub_cells, 0)
    weighted = (own_root[None, :] * (columns.astype(jnp.float32) - mean[None, :])).astype(
        jnp.bfloat16
    )
    partial_gram = gram_local(weighted) / cells
    row_sums = lax.psum_scatter(
        partial_gram.astype(jnp.bfloat16), "tm", scatter_dimension=0, tiled=True
    )
    gram = lax.psum_scatter(row_sums, "space", scatter_dimension=0, tiled=True).astype(jnp.float32)
    inv_root = 1.0 / jnp.sqrt(eigvals)
    projected = jnp.dot(eigvecs.T, weighted, preferred_element_type=jnp.float32)
    mode_piece = (projected * inv_root[:, None]).astype(jnp.bfloat16)
    modes = lax.all_to_all(mode_piece, "tm", split_axis=0, concat_axis=1, tiled=True)
    return (gram, modes)


def solution(mesh):
    in_specs = (P("tm", "space"), P("space"), P(), P())
    out_specs = (P(("tm", "space"), None), P("tm", "space"))
    return jax.shard_map(local, mesh=mesh, in_specs=in_specs, out_specs=out_specs, check_vma=False)
```

profile of v0, /device:TPU:0, one launch (start us, length us, event | category | flops | bytes accessed | tf_op | source)
XLA Modules:
  0.0 484.4 jit_solution(10182316372493514832)
XLA Ops:
  7.2 0.0 copy-start
  7.2 16.6 %copy.8 = bf16[128,49152]{0,1:T(8,128)(2,1)} copy(bf16[128,49152]{1,0:T(8,128)(2,1)} %param.4) | data formatting | bytes 25165824 | tf_op args[0]
  23.8 0.0 copy-start.1
  23.8 6.5 %all-to-all-start = ((bf16[128,4,12288]{0,2,1:T(8,128)(2,1)}), bf16[128,4,12288]{0,2,1:T(8,128)(2,1)}, u32[]{:S(2)}, u32[]{:S(2)}) async-start(bf16[128,4,12288]{0,2,1:T(8,128)(2,1)} %bitcast.22), calls=%async_computation | async-start | bytes 25165824 | tf_op jit(solution)/shard_map/all_to_all | solution.py:21
  30.4 0.0 copy-done.1
  30.4 0.8 dynamic-slice_sqrt_fusion
  31.2 273.7 %all-to-all-done = bf16[128,4,12288]{0,2,1:T(8,128)(2,1)} async-done(((bf16[128,4,12288]{0,2,1:T(8,128)(2,1)}), bf16[128,4,12288]{0,2,1:T(8,128)(2,1)}, u32[]{:S(2)}, u32[]{:S(2)}) %all-to-all-start) | async-done | bytes 12582944 | tf_op jit(solution)/shard_map/all_to_all | solution.py:21
  304.9 6.8 %convert_reduce_fusion = f32[12288]{0:T(1024)S(1)} fusion(bf16[128,4,12288]{0,2,1:T(8,128)(2,1)} %all-to-all-done), kind=kLoop, calls=%fused_computation.2 | loop fusion | flops 12570624 | bytes 12632064 | tf_op jit(solution)/shard_map/reduce_sum | solution.py:22
  311.7 11.7 %fusion.5 = bf16[4,128,12288]{1,2,0:T(8,128)(2,1)} fusion(bf16[128,4,12288]{0,2,1:T(8,128)(2,1)} %all-to-all-done, f32[12288]{0:T(1024)S(1)} %broadcast_multiply_fusion, f32[12288]{0:T(1024)S(1)} %dynamic-slice_sqrt_fusion), kind=kLoop, calls=%fused_computation.10 | loop fusion | flops 25165824 | bytes 25264128 | tf_op jit(solution)/shard_map/mul | solution.py:25
  323.5 16.7 %copy.9 = bf16[4,128,12288]{2,1,0:T(8,128)(2,1)} copy(bf16[4,128,12288]{1,2,0:T(8,128)(2,1)} %fusion.5) | data formatting | bytes 25165824 | tf_op jit(solution)/shard_map/mul | solution.py:25
  340.2 13.9 %convert_bitcast_fusion = f32[4,128,12288]{1,2,0:T(8,128)} fusion(bf16[128,4,12288]{0,2,1:T(8,128)(2,1)} %all-to-all-done), kind=kLoop, calls=%fused_computation | loop fusion | flops 6291456 | bytes 37748736 | tf_op jit(solution)/shard_map/convert_element_type | solution.py:25
  354.0 24.6 %copy.10 = f32[4,128,12288]{2,1,0:T(8,128)} copy(f32[4,128,12288]{1,2,0:T(8,128)} %convert_bitcast_fusion) | data formatting | bytes 50331648 | tf_op jit(solution)/shard_map/convert_element_type | solution.py:25
  378.7 10.0 %fusion.3 = bf16[512,12288]{1,0:T(8,128)(2,1)S(1)} fusion(f32[4,128,12288]{2,1,0:T(8,128)} %copy.10, f32[12288]{0:T(1024)S(1)} %broadcast_multiply_fusion, f32[12288]{0:T(1024)S(1)} %dynamic-slice_sqrt_fusion), kind=kLoop, calls=%fused_computation.7 | loop fusion | flops 18874368 | bytes 37847040 | tf_op jit(solution)/shard_map/convert_element_type | solution.py:25
  388.7 0.0 copy-done
  388.7 3.5 fusion.4
  392.2 3.6 all-to-all-start.1
  395.8 0.0 reduce-scatter.3.cloned.1.call-start
  395.8 15.6 %fusion.6 = bf16[512,512]{1,0:T(8,128)(2,1)} fusion(bf16[512,12288]{1,0:T(8,128)(2,1)} %bitcast.23), kind=kOutput, calls=%fused_computation.12 | convolution fusion | flops 6442975232 | bytes 13107200 | tf_op jit(solution)/shard_map/dot_general | solution.py:8
  411.4 0.0 reduce-scatter.3.cloned.1.call-update
  411.4 0.0 reduce-scatter.5.cloned.1.call-start
  411.5 26.8 %reduce-scatter.3.cloned.1.call-done = bf16[128,512]{1,0:T(8,128)(2,1)} async-done(((bf16[512,512]{1,0:T(8,128)(2,1)}), bf16[128,512]{1,0:T(8,128)(2,1)}) %reduce-scatter.3.cloned.1.call-update) | async-done | bytes 131088 | tf_op jit(solution)/shard_map/reduce_scatter | solution.py:29
  438.2 0.0 reduce-scatter.5.cloned.1.call-update
  438.3 36.7 %reduce-scatter.5.cloned.1.call-done = bf16[16,512]{1,0:T(8,128)(2,1)} async-done(((bf16[128,512]{1,0:T(8,128)(2,1)}), bf16[16,512]{1,0:T(8,128)(2,1)}) %reduce-scatter.5.cloned.1.call-update) | async-done | bytes 16400 | tf_op jit(solution)/shard_map/reduce_scatter | solution.py:32
  475.0 1.3 convert_element_type.38
  476.3 0.0 all-to-all-done.1
  476.3 1.3 copy.12
  (2 shorter events, 0.0 us)
Async XLA Ops:
  7.2 381.5 %copy-start = (bf16[512,64]{0,1:T(8,128)(2,1)S(1)}, bf16[512,64]{0,1:T(8,128)(2,1)}, u32[]{:S(2)}) copy-start(bf16[512,64]{0,1:T(8,128)(2,1)} %param.6) | copy-start | bytes 196612
  23.8 6.6 %copy-start.1 = (f32[64]{0:T(128)S(1)}, f32[64]{0:T(128)}, u32[]{:S(2)}) copy-start(f32[64]{0:T(128)} %param.7) | copy-start | bytes 772
  23.8 281.1 %all-to-all-start = ((bf16[128,4,12288]{0,2,1:T(8,128)(2,1)}), bf16[128,4,12288]{0,2,1:T(8,128)(2,1)}, u32[]{:S(2)}, u32[]{:S(2)}) async-start(bf16[128,4,12288]{0,2,1:T(8,128)(2,1)} %bitcast.22), calls=%async_computation | async-start | bytes 25165824 | tf_op jit(solution)/shard_map/all_to_all | solution.py:21
  392.2 84.1 %all-to-all-start.1 = ((bf16[4,16,12288]{2,1,0:T(8,128)(2,1)}), bf16[4,16,12288]{2,1,0:T(8,128)(2,1)S(1)}, u32[]{:S(2)}, u32[]{:S(2)}) async-start(bf16[4,16,12288]{2,1,0:T(8,128)(2,1)} %bitcast.6), calls=%async_computation.3 | async-start | bytes 3145728 | tf_op jit(solution)/shard_map/all_to_all | solution.py:36
  395.8 42.5 %reduce-scatter.3.cloned.1.call-start = ((), (), s32[]{:S(2)}) async-start(), calls=%async_computation.4 | async-start | bytes 655360 | tf_op jit(solution)/shard_map/reduce_scatter | solution.py:29
  411.4 63.6 %reduce-scatter.5.cloned.1.call-start = ((), (), s32[]{:S(2)}) async-start(), calls=%async_computation.5 | async-start | bytes 147456 | tf_op jit(solution)/shard_map/reduce_scatter | solution.py:32
Sparse Core Ops, SparseCore 0:
  411.5 26.6 reduce-scatter.2
  441.2 33.6 reduce-scatter.4
where the time goes:
time: 486 us; the launch traced here: 484 us
  waiting for transfers between devices  337 us (69%)
  local copies, waits for them, and re-layouts  60.1 us (12%)
  other arithmetic  43.7 us (9%)
  matrix products  19.1 us (4%)
  between operations  14.1 us (3%)
  starting transfers between devices  10.2 us (2%)
    all_to_all x1, waiting for transfers between devices, local(): lax.all_to_all(snapshots, 'tm', split_axis=1, concat_axis=0, tiled=True)  274 us
    reduce_scatter x1, waiting for transfers between devices, local(): lax.psum_scatter(row_sums, 'space', scatter_dimension=0, tiled=True)  36.7 us
    reduce_scatter x1, waiting for transfers between devices, local(): lax.psum_scatter(partial_gram.astype(jnp.bfloat16), 'tm', scatter_dimensi...  26.8 us
    convert_element_type x1, local copies, waits for them, and re-layouts, local(): columns.astype(jnp.float32) - mean[None, :]  24.6 us
    mul x1, local copies, waits for them, and re-layouts, local(): own_root[None, :] * (columns.astype(jnp.float32) - mean[None, :])  16.7 us
    unnamed x5, local copies, waits for them, and re-layouts  16.7 us
    dot_general x1, matrix products, gram_local(): lax.dot_general(weighted, weighted, (((1,), (1,)), ((), ())), preferred_e...  15.6 us
    convert_element_type x1, other arithmetic, local(): columns.astype(jnp.float32) - mean[None, :]  13.9 us
  transfers between devices with their start and end apart: 4, of which 3 were waited for; matrix products, arithmetic and copies ran while one was open for 4% of the time, Pallas kernels for 0%

commit v1 on v0

--- a/solution.py
+++ b/solution.py
@@ -18,7 +18,10 @@
     cells = cell_dev * space_count
     sub_cells = cell_dev // tm_count
     tm_index = lax.axis_index("tm")
-    columns = lax.all_to_all(snapshots, "tm", split_axis=1, concat_axis=0, tiled=True)
+    columns = jnp.concatenate(
+        lax.all_to_all(jnp.stack(jnp.split(snapshots, lax.axis_size("tm"), axis=1)), "tm", 0, 0),
+        axis=0,
+    )
     mean = jnp.sum(columns.astype(jnp.float32), axis=0) / times
     root = jnp.sqrt(area_weight)
     own_root = lax.dynamic_slice_in_dim(root, tm_index * sub_cells, sub_cells, 0)

time: 486 us -> 410 us (0.84)
  local copies, waits for them, and re-layouts: 60.1 us -> 7.3 us
  other arithmetic: 43.7 us -> 29.4 us
  matrix products: 19.1 us -> 10.9 us
    convert_element_type x1 -> x0, local copies, waits for them, and re-layouts: 24.6 us -> none  [local(): columns.astype(jnp.float32) - mean[None, :]]
    mul x1 -> x0, local copies, waits for them, and re-layouts: 16.7 us -> none  [local(): own_root[None, :] * (columns.astype(jnp.float32) - mean[None, :])]
    unnamed x5 -> x6, local copies, waits for them, and re-layouts: 16.7 us -> 0.02 us
    convert_element_type x1 -> x0, other arithmetic: 13.9 us -> none  [local(): columns.astype(jnp.float32) - mean[None, :]]
    mul x1 -> x0, other arithmetic: 11.7 us -> none  [local(): own_root[None, :] * (columns.astype(jnp.float32) - mean[None, :])]
    dot_general x1, matrix products: 15.6 us -> 7.46 us  [gram_local(): lax.dot_general(weighted, weighted, (((1,), (1,)), ((), ())), preferred_e...]
    another operation x0 -> x1, other arithmetic: none -> 5.5 us  [local(): jnp.stack(jnp.split(snapshots, lax.axis_size('tm'), axis=1))]
    another operation x0 -> x1, local copies, waits for them, and re-layouts: none -> 5.2 us  [local(): jnp.stack(jnp.split(snapshots, lax.axis_size('tm'), axis=1))]
where the time goes in v1:
time: 410 us
  waiting for transfers between devices  337 us (82%)
  other arithmetic  29.4 us (7%)
  between operations  14.1 us (3%)
  matrix products  10.9 us (3%)
  starting transfers between devices  10.3 us (3%)
  local copies, waits for them, and re-layouts  7.3 us (2%)
    all_to_all x1, waiting for transfers between devices, local(): lax.all_to_all(jnp.stack(jnp.split(snapshots, lax.axis_size('tm'), axis=1...  274 us
    reduce_scatter x1, waiting for transfers between devices, local(): lax.psum_scatter(row_sums, 'space', scatter_dimension=0, tiled=True)  36.4 us
    reduce_scatter x1, waiting for transfers between devices, local(): lax.psum_scatter(partial_gram.astype(jnp.bfloat16), 'tm', scatter_dimensi...  27.2 us
    convert_element_type x2, other arithmetic, local(): (own_root[None, :] * (columns.astype(jnp.float32) - mean[None, :])).astyp...  14.9 us
  transfers between devices with their start and end apart: 4, of which 3 were waited for; matrix products, arithmetic and copies ran while one was open for 4% of the time, Pallas kernels for 0%

profile of v1, /device:TPU:0, one launch (start us, length us, event | category | flops | bytes accessed | tf_op | source)
XLA Modules:
  0.0 409.5 jit_solution(1710001234131609638)
XLA Ops:
  7.2 0.0 copy-start
  7.2 5.2 %slice_bitcast_fusion.3 = (bf16[1,128,12288]{2,1,0:T(8,128)(2,1)S(1)}, bf16[1,128,12288]{2,1,0:T(8,128)(2,1)S(1)}, bf16[1,128,12288]{2,1,0:T(8,128)(2,1)S(1)}, bf16[1,128,12288]{2,1,0:T(8,128)(2,1)S(1)}) fusion(bf16[128,49152]{1,0:T(8,128)(2,1)} %param.4), kind=kLoop, calls=%fused_computation.11 | loop fusion | bytes 25165824 | tf_op jit(solution)/shard_map/stack | solution.py:22
  12.4 5.5 %pad_maximum_fusion = bf16[4,128,12288]{2,1,0:T(8,128)(2,1)} fusion(bf16[1,128,12288]{2,1,0:T(8,128)(2,1)S(1)} %get-tuple-element.4, bf16[1,128,12288]{2,1,0:T(8,128)(2,1)S(1)} %get-tuple-element.5, bf16[1,128,12288]{2,1,0:T(8,128)(2,1)S(1)} %get-tuple-element.3, bf16[1,128,12288]{2,1,0:T(8,128)(2,1)S(1)} %get-tuple-element.2), kind=kLoop, calls=%fused_computation.6 | loop fusion | flops 18874368 | bytes 25165824 | tf_op jit(solution)/shard_map/stack | solution.py:22
  17.9 0.0 copy-start.2
  17.9 6.5 %all-to-all-start = ((bf16[4,128,12288]{2,1,0:T(8,128)(2,1)}), bf16[4,128,12288]{2,1,0:T(8,128)(2,1)}, u32[]{:S(2)}, u32[]{:S(2)}) async-start(bf16[4,128,12288]{2,1,0:T(8,128)(2,1)} %pad_maximum_fusion), calls=%async_computation | async-start | bytes 25165824 | tf_op jit(solution)/shard_map/all_to_all | solution.py:22
  24.4 0.0 copy-done.2
  24.4 0.8 dynamic-slice_sqrt_fusion
  25.2 273.9 %all-to-all-done = bf16[4,128,12288]{2,1,0:T(8,128)(2,1)} async-done(((bf16[4,128,12288]{2,1,0:T(8,128)(2,1)}), bf16[4,128,12288]{2,1,0:T(8,128)(2,1)}, u32[]{:S(2)}, u32[]{:S(2)}) %all-to-all-start) | async-done | bytes 12582944 | tf_op jit(solution)/shard_map/all_to_all | solution.py:22
  299.1 7.7 %convert_reduce_fusion = f32[12288]{0:T(1024)S(1)} fusion(bf16[4,128,12288]{2,1,0:T(8,128)(2,1)} %all-to-all-done), kind=kLoop, calls=%fused_computation.7 | loop fusion | flops 12570624 | bytes 12632064 | tf_op jit(solution)/shard_map/reduce_sum | solution.py:25
  306.8 7.4 %fusion.1 = bf16[512,12288]{1,0:T(8,128)(2,1)S(1)} fusion(f32[12288]{0:T(1024)S(1)} %broadcast_multiply_fusion, f32[12288]{0:T(1024)S(1)} %dynamic-slice_sqrt_fusion, bf16[4,128,12288]{2,1,0:T(8,128)(2,1)} %all-to-all-done), kind=kLoop, calls=%fused_computation.2 | loop fusion | flops 25165824 | bytes 25264128 | tf_op jit(solution)/shard_map/convert_element_type | solution.py:28
  314.3 0.0 copy-done
  314.3 3.5 fusion.2
  317.7 3.6 all-to-all-start.1
  321.3 0.2 reduce-scatter.3.cloned.1.call-start
  321.6 7.4 %multiply_convert_fusion = bf16[4,128,12288]{2,1,0:T(8,128)(2,1)S(1)} fusion(f32[12288]{0:T(1024)S(1)} %broadcast_multiply_fusion, bf16[4,128,12288]{2,1,0:T(8,128)(2,1)} %all-to-all-done, f32[12288]{0:T(1024)S(1)} %dynamic-slice_sqrt_fusion), kind=kLoop, calls=%fused_computation.3 | loop fusion | flops 25165824 | bytes 25264128 | tf_op jit(solution)/shard_map/convert_element_type | solution.py:28
  329.0 0.0 copy-start.1
  329.0 7.5 %fusion.3 = bf16[512,512]{1,0:T(8,128)(2,1)} fusion(bf16[512,12288]{1,0:T(8,128)(2,1)S(1)} %bitcast.25), kind=kOutput, calls=%fused_computation.13 | convolution fusion | flops 6442975232 | bytes 13107200 | tf_op jit(solution)/shard_map/dot_general | solution.py:8
  336.5 0.0 reduce-scatter.3.cloned.1.call-update
  336.5 0.0 reduce-scatter.5.cloned.1.call-start
  336.5 27.2 %reduce-scatter.3.cloned.1.call-done = bf16[128,512]{1,0:T(8,128)(2,1)} async-done(((bf16[512,512]{1,0:T(8,128)(2,1)}), bf16[128,512]{1,0:T(8,128)(2,1)}) %reduce-scatter.3.cloned.1.call-update) | async-done | bytes 131088 | tf_op jit(solution)/shard_map/reduce_scatter | solution.py:32
  363.7 0.0 reduce-scatter.5.cloned.1.call-update
  363.7 36.4 %reduce-scatter.5.cloned.1.call-done = bf16[16,512]{1,0:T(8,128)(2,1)} async-done(((bf16[128,512]{1,0:T(8,128)(2,1)}), bf16[16,512]{1,0:T(8,128)(2,1)}) %reduce-scatter.5.cloned.1.call-update) | async-done | bytes 16400 | tf_op jit(solution)/shard_map/reduce_scatter | solution.py:35
  400.1 1.3 convert_element_type.37
  401.4 0.0 all-to-all-done.1
  401.4 1.3 copy.7
  402.7 0.0 copy-done.1
  (2 shorter events, 0.0 us)
Async XLA Ops:
  7.2 307.1 %copy-start = (bf16[512,64]{0,1:T(8,128)(2,1)S(1)}, bf16[512,64]{0,1:T(8,128)(2,1)}, u32[]{:S(2)}) copy-start(bf16[512,64]{0,1:T(8,128)(2,1)} %param.6) | copy-start | bytes 196612
  17.9 6.5 %copy-start.2 = (f32[64]{0:T(128)S(1)}, f32[64]{0:T(128)}, u32[]{:S(2)}) copy-start(f32[64]{0:T(128)} %param.7) | copy-start | bytes 772
  17.9 281.2 %all-to-all-start = ((bf16[4,128,12288]{2,1,0:T(8,128)(2,1)}), bf16[4,128,12288]{2,1,0:T(8,128)(2,1)}, u32[]{:S(2)}, u32[]{:S(2)}) async-start(bf16[4,128,12288]{2,1,0:T(8,128)(2,1)} %pad_maximum_fusion), calls=%async_computation | async-start | bytes 25165824 | tf_op jit(solution)/shard_map/all_to_all | solution.py:22
  317.7 83.7 %all-to-all-start.1 = ((bf16[4,16,12288]{2,1,0:T(8,128)(2,1)}), bf16[4,16,12288]{2,1,0:T(8,128)(2,1)S(1)}, u32[]{:S(2)}, u32[]{:S(2)}) async-start(bf16[4,16,12288]{2,1,0:T(8,128)(2,1)} %bitcast.27), calls=%async_computation.3 | async-start | bytes 3145728 | tf_op jit(solution)/shard_map/all_to_all | solution.py:39
  321.3 42.4 %reduce-scatter.3.cloned.1.call-start = ((), (), s32[]{:S(2)}) async-start(), calls=%async_computation.4 | async-start | bytes 655360 | tf_op jit(solution)/shard_map/reduce_scatter | solution.py:32
  329.0 73.7 %copy-start.1 = (bf16[512,64]{0,1:T(8,128)(2,1)S(1)}, bf16[512,64]{0,1:T(8,128)(2,1)}, u32[]{:S(2)}) copy-start(bf16[512,64]{0,1:T(8,128)(2,1)} %param.6) | copy-start | bytes 196612
  336.5 63.6 %reduce-scatter.5.cloned.1.call-start = ((), (), s32[]{:S(2)}) async-start(), calls=%async_computation.5 | async-start | bytes 147456 | tf_op jit(solution)/shard_map/reduce_scatter | solution.py:35
Sparse Core Ops, SparseCore 0:
  336.6 27.0 reduce-scatter.2
  366.7 33.3 reduce-scatter.4
